TPU v7x, 32 devices: a whole 2x2x4 slice. The times are simulated.
32 devices in a mesh: expert: 4 (over y, x), dp: 8 (over z, core).
Axes of the slice: x: 2, y: 2, z: 4, core: 2. Of those that a mesh axis runs over, the one named last changes fastest.
Arguments:
- gradient: bfloat16 [4, 8, 32, 4096], P('expert', 'dp'), may hold values from -6700 to 6700
- momentum: float32 [4, 32, 4096], P('expert'), may hold values from -4 to 4
- variance: bfloat16 [4, 32, 4096], P('expert'), may hold values from 0.0099487305 to 1
- worker_error: float32 [4, 8, 32, 4096], P('expert', 'dp'), may hold values from -6 to 6
- server_error: float32 [4, 32, 4096], P('expert', 'dp'), may hold values from -4 to 4
Outputs:
- new_momentum: float32 [4, 32, 4096], P('expert')
- adam_step: bfloat16 [4, 32, 4096], P('expert')
- new_worker_error: float32 [4, 8, 32, 4096], P('expert', 'dp')
- new_server_error: float32 [4, 32, 4096], P('expert', 'dp')
All inputs are finite; a program needn't handle non-finite values. Where the computation divides by a largest or mean magnitude, that divisor is 1e-20 or more.
Results may differ from a plain program's by a relative error of at most 0.011.
Values may be sent and summed in bfloat16 or wider, within the bound.
No kernel may reach another device: no remote copies, remote signals or barrier semaphores. Data moves between devices by JAX's collectives and lax.ppermute only.
A program may use at most 128 MiB of HBM per device.

v0:
```python
import functools
import math

import jax
import jax.numpy as jnp
from jax import lax
from jax.experimental import pallas as pl
from jax.experimental.pallas import tpu as pltpu
from jax.sharding import PartitionSpec as P


beta_one = 0.9
rms_limit = 5.0
scale_eps = 1e-06
adam_eps = 1e-08
CORES = 2
LANE_ROWS, LANES = 8, 128
VMEM_LIMIT = 16 << 20


def stage_sizes(count):
    sizes = []
    for radix in (2, 4, 4, 4, 4):
        if count % radix == 0:
            sizes.append(radix)
            count //= radix
    for radix in range(2, count + 1):
        while count % radix == 0:
            sizes.append(radix)
            count //= radix
    return sizes


def partner(index, step, stride, radix):
    digit = (index // stride) % radix
    other = digit ^ step if radix & (radix - 1) == 0 else (digit + step) % radix
    return index + (other - digit) * stride


def swap(values, axis, step, stride, radix, count):
    pairs = [(i, partner(i, step, stride, radix)) for i in range(count)]
    return lax.ppermute(values, axis, pairs)


def peer_digit(digit, step, radix, back=False):
    if radix & (radix - 1) == 0:
        return digit ^ step
    return (digit + (radix - step if back else step)) % radix


def expert_sum(part):
    count = lax.axis_size("expert")
    total = part
    for step in range(1, count):
        total = total + swap(part, "expert", step, 1, count, count)
    return total


def compress(values):
    row_scale = jnp.mean(jnp.abs(values), axis=-1, keepdims=True).astype(jnp.bfloat16).astype(jnp.float32)
    row_code = jnp.clip(values / (row_scale + scale_eps), -1.0, 1.0).astype(jnp.bfloat16)
    return row_scale * row_code.astype(jnp.float32)


def scatter_sum(rows, replicas, group_rows):
    width = rows.shape[-1]
    place = lax.axis_index("dp")
    stride = 1
    held = rows.reshape(replicas, group_rows, width)
    for radix in stage_sizes(replicas):
        digit = (place // stride) % radix
        blocks = held.reshape(held.shape[0] // radix, radix, group_rows, width)
        total = lax.dynamic_index_in_dim(blocks, digit, 1, keepdims=False)
        for step in range(1, radix):
            piece = lax.dynamic_index_in_dim(blocks, peer_digit(digit, step, radix), 1, keepdims=False)
            got = swap(piece.astype(jnp.bfloat16), "dp", step, stride, radix, replicas)
            total = total + got.astype(jnp.float32)
        held = total
        stride *= radix
    return held[0]


def gather_rows(own, replicas):
    group_rows, width = own.shape
    place = lax.axis_index("dp")
    held = own[None]
    stride = replicas
    for radix in reversed(stage_sizes(replicas)):
        stride //= radix
        digit = (place // stride) % radix
        blocks = jnp.zeros((held.shape[0], radix) + own.shape, own.dtype)
        blocks = lax.dynamic_update_index_in_dim(blocks, held, digit, 1)
        for step in range(1, radix):
            got = swap(held, "dp", step, stride, radix, replicas)
            blocks = lax.dynamic_update_index_in_dim(blocks, got, peer_digit(digit, step, radix, True), 1)
        held = blocks.reshape(held.shape[0] * radix, group_rows, width)
    return held.reshape(replicas * group_rows, width)


def per_device(gradient, momentum, variance, worker_error, server_error):
    grad_local = gradient[0, 0].astype(jnp.float32)
    squares = expert_sum(jnp.sum(jnp.square(grad_local)).reshape(1, 1))
    entry_count = lax.axis_size("expert") * grad_local.shape[0] * grad_local.shape[1]
    root_mean = jnp.sqrt(squares / entry_count + 1e-06)
    clip_factor = jnp.minimum(1.0, rms_limit / root_mean)
    clipped = grad_local * clip_factor
    compensated = beta_one * momentum[0] + (1.0 - beta_one) * clipped + worker_error[0, 0]
    decoded = compress(compensated)
    worker_new = compensated - decoded
    replicas = lax.axis_size("dp")
    group_rows = server_error.shape[1]
    average = scatter_sum(decoded, replicas, group_rows) / replicas
    combined = average + server_error[0]
    owner_decoded = compress(combined)
    server_new = combined - owner_decoded
    momentum_new = gather_rows(owner_decoded.astype(jnp.bfloat16), replicas).astype(jnp.float32)
    step_out = (momentum_new / (jnp.sqrt(variance[0].astype(jnp.float32)) + adam_eps)).astype(
        jnp.bfloat16
    )
    return (momentum_new[None], step_out[None], worker_new[None, None], server_new[None])


def kernel_call(body, outs, operands, scratch=(), out_space=None, in_space=None, aliases=None, flops=0):
    bytes_moved = sum(x.size * x.dtype.itemsize for x in operands) + sum(
        math.prod(shape) * jnp.dtype(kind).itemsize for shape, kind in outs
    )
    spaces = in_space or [pltpu.VMEM] * len(operands)
    out_spaces = out_space or [pltpu.VMEM] * len(outs)
    return pl.pallas_call(
        body,
        out_shape=[jax.ShapeDtypeStruct(shape, kind) for shape, kind in outs],
        in_specs=[pl.BlockSpec(memory_space=space) for space in spaces],
        out_specs=[pl.BlockSpec(memory_space=space) for space in out_spaces],
        scratch_shapes=list(scratch),
        input_output_aliases=aliases or {},
        compiler_params=pltpu.CompilerParams(vmem_limit_bytes=VMEM_LIMIT),
        cost_estimate=pl.CostEstimate(flops=flops, bytes_accessed=bytes_moved, transcendentals=0),
    )(*operands)


def squares_kernel(grad_ref, out_ref):
    rows, width = grad_ref.shape
    total = [jnp.zeros((LANE_ROWS, LANES), jnp.float32) for _ in range(4)]
    turn = 0
    for row in range(0, rows, LANE_ROWS):
        for column in range(0, width, LANES):
            piece = grad_ref[row : row + LANE_ROWS, column : column + LANES].astype(jnp.float32)
            total[turn % 4] = total[turn % 4] + piece * piece
            turn += 1
    out_ref[...] = (total[0] + total[1]) + (total[2] + total[3])


def base_kernel(momentum_ref, error_ref, base_ref):
    for row in range(0, base_ref.shape[0], LANE_ROWS):
        rows = slice(row, row + LANE_ROWS)
        base_ref[rows, :] = beta_one * momentum_ref[rows, :] + error_ref[rows, :]


def row_scale_of(values):
    mean = jnp.sum(jnp.abs(values), axis=-1, keepdims=True) / values.shape[-1]
    return mean.astype(jnp.bfloat16).astype(jnp.float32)


def coded(values, scale):
    code = jnp.clip(values * (1.0 / (scale + scale_eps)), -1.0, 1.0).astype(jnp.bfloat16)
    return scale * code.astype(jnp.float32)


def position():
    place = lax.axis_index("dp")
    return place // CORES, place % CORES == 0


def chip_rows_at(chip, chip_rows):
    return pl.ds(pl.multiple_of(chip * chip_rows, chip_rows), chip_rows)


def pick_half(low, high, top):
    half = low.shape[0] // CORES
    return jnp.where(
        top, jnp.concatenate([low[:half], high[:half]]), jnp.concatenate([low[half:], high[half:]])
    )


def worker_kernel(experts, chip_rows, *refs):
    parts = refs[:experts]
    grad_ref, base_ref, same_ref, cross_ref, send_ref, scale_ref, sum_ref = refs[experts:]
    total = parts[0][...]
    for part in parts[1:]:
        total = total + part[...]
    count = experts * grad_ref.shape[0] * grad_ref.shape[1]
    squares = jnp.sum(total, axis=(0, 1), keepdims=True)
    factor = jnp.minimum(1.0, rms_limit / jnp.sqrt(squares / count + 1e-06))
    chip, first = position()
    for turn, mine_ref in enumerate((same_ref, cross_ref)):
        parity = (chip + turn) % 2
        decoded = []
        for block in (parity, parity + 2):
            rows = chip_rows_at(block, chip_rows)
            values = base_ref[rows, :] + (1.0 - beta_one) * (grad_ref[rows, :].astype(jnp.float32) * factor)
            sum_ref[rows, :] = values
            scale = row_scale_of(values)
            scale_ref[rows, :] = jnp.broadcast_to(scale, (chip_rows, LANES))
            decoded.append(coded(values, scale))
        mine_ref[...] = pick_half(*decoded, first)
        send_ref[turn * chip_rows : (turn + 1) * chip_rows, :] = pick_half(*decoded, jnp.logical_not(first)).astype(
            jnp.bfloat16
        )


def worker_error_kernel(chip_rows, scale_ref, sum_ref, variance_ref, new_hbm, inverse_ref, new_ref, sems):
    copies = []
    chunks = [slice(row, row + chip_rows) for row in range(0, sum_ref.shape[0], chip_rows)]
    for i, rows in enumerate(chunks):
        values = sum_ref[rows, :]
        new_ref[rows, :] = values - coded(values, scale_ref[rows, 0:1])
        copies.append(pltpu.make_async_copy(new_ref.at[rows, :], new_hbm.at[rows, :], sems.at[i]))
        copies[-1].start()
    for rows in chunks:
        inverse_ref[rows, :] = 1.0 / (jnp.sqrt(variance_ref[rows, :].astype(jnp.float32)) + adam_eps)
    for copy in copies:
        copy.wait()


def chip_sum_kernel(replicas, chip_rows, same_ref, cross_ref, got_ref, error_ref, same_out, cross_out):
    chip, _ = position()
    error = replicas * error_ref[...]
    none = jnp.zeros_like(error)
    owned = jnp.where(chip < 2, jnp.concatenate([error, none]), jnp.concatenate([none, error]))
    same_out[...] = (same_ref[...] + got_ref[:chip_rows, :].astype(jnp.float32) + owned).astype(jnp.bfloat16)
    cross_out[...] = (cross_ref[...] + got_ref[chip_rows:, :].astype(jnp.float32)).astype(jnp.bfloat16)


def owner_kernel(replicas, own_ref, near_ref, far_ref, across_ref, sum_ref, out_ref):
    own, near, far, across = (ref[...].astype(jnp.float32) for ref in (own_ref, near_ref, far_ref, across_ref))
    values = ((own + across) + (near + far)) / replicas
    sum_ref[...] = values
    out_ref[...] = coded(values, row_scale_of(values)).astype(jnp.bfloat16)


def server_error_kernel(sum_ref, new_ref):
    values = sum_ref[...]
    left = values - coded(values, row_scale_of(values))
    half = left.shape[0] // CORES
    chip, _ = position()
    new_ref[...] = jnp.where(chip < 2, left[:half], left[half:])


def result_kernel(chip_rows, turn, mine_ref, other_ref, inverse_ref, *refs):
    momentum_ref, step_ref, momentum_buf, step_buf, sems = refs[-5:]
    chip, first = position()
    parity = (chip + turn) % 2
    mine, other = mine_ref[...].astype(jnp.float32), other_ref[...].astype(jnp.float32)
    half = chip_rows // CORES
    copies = []
    for slot in range(2):
        part = slice(slot * half, (slot + 1) * half)
        values = jnp.where(
            first, jnp.concatenate([mine[part], other[part]]), jnp.concatenate([other[part], mine[part]])
        )
        rows = chip_rows_at(parity + 2 * slot, chip_rows)
        momentum_buf[slot] = values
        copies.append(pltpu.make_async_copy(momentum_buf.at[slot], momentum_ref.at[rows, :], sems.at[0, slot]))
        copies[-1].start()
        step_buf[slot] = (values * inverse_ref[rows, :]).astype(jnp.bfloat16)
        copies.append(pltpu.make_async_copy(step_buf.at[slot], step_ref.at[rows, :], sems.at[1, slot]))
        copies[-1].start()
    for copy in copies:
        copy.wait()


def result_rows(chip_rows, turn, mine, other, inverse, outs):
    rows, width = inverse.shape
    shapes = [((rows, width), jnp.float32), ((rows, width), jnp.bfloat16)]
    return kernel_call(
        functools.partial(result_kernel, chip_rows, turn),
        shapes,
        [mine, other, inverse, *outs],
        in_space=[pltpu.VMEM] * 3 + [pltpu.HBM] * len(outs),
        out_space=[pltpu.HBM] * 2,
        scratch=[
            pltpu.VMEM((2, chip_rows, width), jnp.float32),
            pltpu.VMEM((2, chip_rows, width), jnp.bfloat16),
            pltpu.SemaphoreType.DMA((2, 2)),
        ],
        aliases={3 + i: i for i in range(len(outs))},
        flops=2 * rows * width,
    )


def per_device_chips(gradient, momentum, variance, worker_error, server_error):
    experts, replicas = lax.axis_size("expert"), lax.axis_size("dp")
    chips = replicas // CORES
    rows, width = gradient.shape[2:]
    chip_rows = rows // chips
    half = server_error.shape[1]
    f32, bf16 = jnp.float32, jnp.bfloat16
    block = (chip_rows, width)
    grad, moment, error = gradient[0, 0], momentum[0], worker_error[0, 0]

    def chip_swap(values, step):
        return swap(values, "dp", step, CORES, chips, replicas)

    def core_swap(values):
        return swap(values, "dp", 1, 1, CORES, replicas)

    (part,) = kernel_call(squares_kernel, [((LANE_ROWS, LANES), f32)], [grad], flops=2 * rows * width)
    parts = [part] + [swap(part, "expert", step, 1, experts, experts) for step in reversed(range(1, experts))]
    (base,) = kernel_call(base_kernel, [((rows, width), f32)], [moment, error], flops=2 * rows * width)
    same, cross, send, scales, sums = kernel_call(
        functools.partial(worker_kernel, experts, chip_rows),
        [(block, f32), (block, f32), ((2 * chip_rows, width), bf16), ((rows, LANES), f32), ((rows, width), f32)],
        parts + [grad, base],
        flops=20 * rows * width,
    )
    got = core_swap(send)
    same_sum, cross_sum = kernel_call(
        functools.partial(chip_sum_kernel, replicas, chip_rows),
        [(block, bf16), (block, bf16)],
        [same, cross, got, server_error[0]],
        flops=4 * rows * width,
    )
    far = chip_swap(cross_sum, 3)
    across = chip_swap(same_sum, 2)
    near = chip_swap(cross_sum, 1)
    worker_new, inverse = kernel_call(
        functools.partial(worker_error_kernel, chip_rows),
        [((rows, width), f32), ((rows, width), f32)],
        [scales, sums, variance[0]],
        out_space=[pltpu.HBM, pltpu.VMEM],
        scratch=[pltpu.VMEM((rows, width), f32), pltpu.SemaphoreType.DMA((chips,))],
        flops=20 * rows * width,
    )
    combined, decoded = kernel_call(
        functools.partial(owner_kernel, replicas),
        [(block, f32), (block, bf16)],
        [same_sum, near, far, across],
        flops=20 * chip_rows * width,
    )
    cross_decoded = chip_swap(decoded, 1)
    cross_pairs = [(i, i ^ (CORES + 1)) for i in range(replicas)]
    other_cross = lax.ppermute(decoded, "dp", cross_pairs)
    other_decoded = core_swap(decoded)
    (server_new,) = kernel_call(server_error_kernel, [((half, width), f32)], [combined], flops=20 * chip_rows * width)
    outs = result_rows(chip_rows, 0, decoded, other_decoded, inverse, ())
    momentum_new, step_out = result_rows(chip_rows, 1, cross_decoded, other_cross, inverse, outs)
    return (momentum_new[None], step_out[None], worker_new[None, None], server_new[None])


def solution(mesh):
    if mesh.shape["dp"] == 4 * CORES:
        return placed_step(mesh, per_device_chips)
    return placed_step(mesh, per_device)


def placed_step(mesh, body):
    placed = (
        P("expert", "dp", None, None),
        P("expert", None, None),
        P("expert", None, None),
        P("expert", "dp", None, None),
        P("expert", "dp", None),
    )
    return jax.shard_map(
        body,
        mesh=mesh,
        in_specs=placed,
        out_specs=(
            P("expert", None, None),
            P("expert", None, None),
            P("expert", "dp", None, None),
            P("expert", "dp", None),
        ),
        check_vma=False,
    )
```

profile of v0, /device:TPU:0, one launch (start us, length us, event | category | flops | bytes accessed | tf_op | source)
XLA Modules:
  0.0 29.0 jit_solution(11803820945593975972)
XLA Ops:
  0.6 0.0 copy-start
  0.6 0.9 %copy-done = bf16[1,1,32,4096]{3,2,1,0:T(8,128)(2,1)S(1)} copy-done((bf16[1,1,32,4096]{3,2,1,0:T(8,128)(2,1)S(1)}, bf16[1,1,32,4096]{3,2,1,0:T(8,128)(2,1)}, u32[]{:S(2)}) %copy-start) | copy-done | bytes 262168
  1.6 3.0 %collective-permute-start.2 = (f32[8,128]{1,0:T(8,128)S(1)}, f32[8,128]{1,0:T(8,128)S(1)}, u32[]{:S(2)}, u32[]{:S(2)}) collective-permute-start(f32[8,128]{1,0:T(8,128)S(1)} %shard_map.84.refs_0_), channel_id=1, source_target_pairs={{0,8},{8,0},{16,24},{24,16},{1,9},{9,1},{17,25},{25,17},{2,10},{10... | collective-permute-start | bytes 12296 | tf_op jit(solution)/shard_map/ppermute | solution.py:42
  4.6 1.5 %collective-permute-start.1 = (f32[8,128]{1,0:T(8,128)S(1)}, f32[8,128]{1,0:T(8,128)S(1)}, u32[]{:S(2)}, u32[]{:S(2)}) collective-permute-start(f32[8,128]{1,0:T(8,128)S(1)} %shard_map.84.refs_0_), channel_id=1, source_target_pairs={{0,16},{8,24},{16,0},{24,8},{1,17},{9,25},{17,1},{25,9},{2,18},{10... | collective-permute-start | bytes 12296 | tf_op jit(solution)/shard_map/ppermute | solution.py:42
  6.2 0.0 collective-permute-start
  6.2 0.0 copy-start.2
  6.2 1.0 %copy-done.2 = f32[1,32,4096]{2,1,0:T(8,128)S(1)} copy-done((f32[1,32,4096]{2,1,0:T(8,128)S(1)}, f32[1,32,4096]{2,1,0:T(8,128)}, u32[]{:S(2)}) %copy-start.2) | copy-done | bytes 524312
  7.2 0.0 copy-start.3
  7.2 1.0 %copy-done.3 = f32[1,1,32,4096]{3,2,1,0:T(8,128)S(1)} copy-done((f32[1,1,32,4096]{3,2,1,0:T(8,128)S(1)}, f32[1,1,32,4096]{3,2,1,0:T(8,128)}, u32[]{:S(2)}) %copy-start.3) | copy-done | bytes 524312
  8.3 0.0 copy-start.1
  8.3 0.1 shard_map.85.refs_5_
  8.3 0.0 copy-start.5
  8.3 0.0 collective-permute-done.2.refs_3_
  8.4 0.0 collective-permute-done.1.refs_2_
  8.4 2.3 %collective-permute-done.refs_1_ = f32[8,128]{1,0:T(8,128)S(1)} collective-permute-done((f32[8,128]{1,0:T(8,128)S(1)}, f32[8,128]{1,0:T(8,128)S(1)}, u32[]{:S(2)}, u32[]{:S(2)}) %collective-permute-start) | collective-permute-done | bytes 4128 | tf_op jit(solution)/shard_map/ppermute | solution.py:42
  10.7 0.0 copy-done.1
  10.7 0.5 %shard_map.86 = (f32[8,4096]{1,0:T(8,128)S(1)}, f32[8,4096]{1,0:T(8,128)S(1)}, bf16[16,4096]{1,0:T(8,128)(2,1)S(1)}, f32[32,128]{1,0:T(8,128)S(1)}, f32[32,4096]{1,0:T(8,128)S(1)}) custom-call(f32[8,128]{1,0:T(8,128)S(1)} %shard_map.84.refs_0_, f32[8,128]{1,0:T(8,128)S(1)} %collective-permute-done.refs_1_, f32[8,128]{1,0:T(8,128)S(1)} %collective-permute-done.1.refs_2_, ...), custom_call_target="tpu_custom_call" | custom-call | flops 2621440 | bytes 1736704 | tf_op jit(solution)/shard_map/pallas_call | solution.py:129
  11.1 0.1 collective-permute-start.3
  11.2 1.3 %collective-permute-done.3.got_ref = bf16[16,4096]{1,0:T(8,128)(2,1)S(1)} collective-permute-done((bf16[16,4096]{1,0:T(8,128)(2,1)S(1)}, bf16[16,4096]{1,0:T(8,128)(2,1)S(1)}, u32[]{:S(2)}, u32[]{:S(2)}) %collective-permute-start.3) | collective-permute-done | bytes 131104 | tf_op jit(solution)/shard_map/ppermute | solution.py:42
  12.6 0.0 copy-done.5
  12.6 0.0 copy-start.4
  12.6 0.1 shard_map.87
  12.6 2.7 %collective-permute-start.6 = (bf16[8,4096]{1,0:T(8,128)(2,1)S(1)}, bf16[8,4096]{1,0:T(8,128)(2,1)S(1)}, u32[]{:S(2)}, u32[]{:S(2)}) collective-permute-start(bf16[8,4096]{1,0:T(8,128)(2,1)S(1)} %get-tuple-element.22.own_ref), channel_id=1, source_target_pairs={{0,4},{1,5},{2,6},{3,7},{4,0},{5,1},{6,2},{7,3},{8,12},{9,13},{10,... | collective-permute-start | bytes 196616 | tf_op jit(solution)/shard_map/ppermute | solution.py:42
  15.3 1.3 %collective-permute-start.5 = (bf16[8,4096]{1,0:T(8,128)(2,1)S(1)}, bf16[8,4096]{1,0:T(8,128)(2,1)S(1)}, u32[]{:S(2)}, u32[]{:S(2)}) collective-permute-start(bf16[8,4096]{1,0:T(8,128)(2,1)S(1)} %get-tuple-element.23), channel_id=1, source_target_pairs={{0,6},{1,7},{2,4},{3,5},{4,2},{5,3},{6,0},{7,1},{8,14},{9,15},{10,... | collective-permute-start | bytes 196616 | tf_op jit(solution)/shard_map/ppermute | solution.py:42
  16.6 0.2 collective-permute-start.4
  16.8 3.5 %collective-permute-done.6.across_ref = bf16[8,4096]{1,0:T(8,128)(2,1)S(1)} collective-permute-done((bf16[8,4096]{1,0:T(8,128)(2,1)S(1)}, bf16[8,4096]{1,0:T(8,128)(2,1)S(1)}, u32[]{:S(2)}, u32[]{:S(2)}) %collective-permute-start.6) | collective-permute-done | bytes 65568 | tf_op jit(solution)/shard_map/ppermute | solution.py:42
  20.4 1.3 %collective-permute-done.5.far_ref = bf16[8,4096]{1,0:T(8,128)(2,1)S(1)} collective-permute-done((bf16[8,4096]{1,0:T(8,128)(2,1)S(1)}, bf16[8,4096]{1,0:T(8,128)(2,1)S(1)}, u32[]{:S(2)}, u32[]{:S(2)}) %collective-permute-start.5) | collective-permute-done | bytes 65568 | tf_op jit(solution)/shard_map/ppermute | solution.py:42
  21.6 0.4 %collective-permute-done.4.near_ref = bf16[8,4096]{1,0:T(8,128)(2,1)S(1)} collective-permute-done((bf16[8,4096]{1,0:T(8,128)(2,1)S(1)}, bf16[8,4096]{1,0:T(8,128)(2,1)S(1)}, u32[]{:S(2)}, u32[]{:S(2)}) %collective-permute-start.4) | collective-permute-done | bytes 65568 | tf_op jit(solution)/shard_map/ppermute | solution.py:42
  22.0 0.2 shard_map.88
  22.2 0.1 collective-permute-start.9
  22.3 0.7 %collective-permute-start.8 = (bf16[8,4096]{1,0:T(8,128)(2,1)S(1)}, bf16[8,4096]{1,0:T(8,128)(2,1)S(1)}, u32[]{:S(2)}, u32[]{:S(2)}) collective-permute-start(bf16[8,4096]{1,0:T(8,128)(2,1)S(1)} %get-tuple-element.24.mine_ref), channel_id=1, source_target_pairs={{0,3},{1,2},{2,1},{3,0},{4,7},{5,6},{6,5},{7,4},{8,11},{9,10},{10,... | collective-permute-start | bytes 196616 | tf_op jit(solution)/shard_map/ppermute | solution.py:342
  23.0 1.4 %collective-permute-start.7 = (bf16[8,4096]{1,0:T(8,128)(2,1)S(1)}, bf16[8,4096]{1,0:T(8,128)(2,1)S(1)}, u32[]{:S(2)}, u32[]{:S(2)}) collective-permute-start(bf16[8,4096]{1,0:T(8,128)(2,1)S(1)} %get-tuple-element.24.mine_ref), channel_id=1, source_target_pairs={{0,2},{1,3},{2,0},{3,1},{4,6},{5,7},{6,4},{7,5},{8,10},{9,11},{10,... | collective-permute-start | bytes 196616 | tf_op jit(solution)/shard_map/ppermute | solution.py:42
  24.4 0.0 copy-done.4
  24.4 0.9 %shard_map.89 = (f32[32,4096]{1,0:T(8,128)}, f32[32,4096]{1,0:T(8,128)S(1)}) custom-call(f32[32,128]{1,0:T(8,128)S(1)} %get-tuple-element.25.scale_ref, f32[32,4096]{1,0:T(8,128)S(1)} %get-tuple-element.26.sum_ref, bf16[32,4096]{1,0:T(8,128)(2,1)S(1)} %bitcast.13), custom_call_target="tpu_custom_call" | custom-call | flops 2621440 | bytes 1851392 | tf_op jit(solution)/shard_map/pallas_call | solution.py:129
  25.4 0.8 %shard_map.92 = f32[4,4096]{1,0:T(4,128)} custom-call(f32[8,4096]{1,0:T(8,128)S(1)} %get-tuple-element.33.sum_ref), custom_call_target="tpu_custom_call" | custom-call | flops 655360 | bytes 196608 | tf_op jit(solution)/shard_map/pallas_call | solution.py:129
  26.1 0.0 collective-permute-done.9.other_ref
  26.2 0.8 %shard_map.90 = (f32[32,4096]{1,0:T(8,128)}, bf16[32,4096]{1,0:T(8,128)(2,1)}) custom-call(bf16[8,4096]{1,0:T(8,128)(2,1)S(1)} %get-tuple-element.24.mine_ref, bf16[8,4096]{1,0:T(8,128)(2,1)S(1)} %collective-permute-done.9.other_ref, f32[32,4096]{1,0:T(8,128)S(1)} %get-tuple-element.27.inverse_ref), custom_call_target="tpu_custom_call" | custom-call | flops 262144 | bytes 1441792 | tf_op jit(solution)/shard_map/pallas_call | solution.py:129
  27.0 0.0 collective-permute-done.8.other_ref
  27.0 1.2 %collective-permute-done.7.mine_ref = bf16[8,4096]{1,0:T(8,128)(2,1)S(1)} collective-permute-done((bf16[8,4096]{1,0:T(8,128)(2,1)S(1)}, bf16[8,4096]{1,0:T(8,128)(2,1)S(1)}, u32[]{:S(2)}, u32[]{:S(2)}) %collective-permute-start.7) | collective-permute-done | bytes 65568 | tf_op jit(solution)/shard_map/ppermute | solution.py:42
  28.2 0.8 %shard_map.91 = (f32[32,4096]{1,0:T(8,128)}, bf16[32,4096]{1,0:T(8,128)(2,1)}) custom-call(bf16[8,4096]{1,0:T(8,128)(2,1)S(1)} %collective-permute-done.7.mine_ref, bf16[8,4096]{1,0:T(8,128)(2,1)S(1)} %collective-permute-done.8.other_ref, f32[32,4096]{1,0:T(8,128)S(1)} %get-tuple-element.27.inverse_ref, ...), custom_call_target="tpu_custom_call", output_to_operand_aliasing={{0}: (3, {}), {1}: (4, {})} | custom-call | flops 262144 | bytes 2228224 | tf_op jit(solution)/shard_map/pallas_call | solution.py:129
  (1 shorter events, 0.0 us)
Async XLA Ops:
  0.6 1.0 %copy-start = (bf16[1,1,32,4096]{3,2,1,0:T(8,128)(2,1)S(1)}, bf16[1,1,32,4096]{3,2,1,0:T(8,128)(2,1)}, u32[]{:S(2)}) copy-start(bf16[1,1,32,4096]{3,2,1,0:T(8,128)(2,1)} %param.5) | copy-start | bytes 786436
  1.6 6.7 %collective-permute-start.2 = (f32[8,128]{1,0:T(8,128)S(1)}, f32[8,128]{1,0:T(8,128)S(1)}, u32[]{:S(2)}, u32[]{:S(2)}) collective-permute-start(f32[8,128]{1,0:T(8,128)S(1)} %shard_map.84.refs_0_), channel_id=1, source_target_pairs={{0,8},{8,0},{16,24},{24,16},{1,9},{9,1},{17,25},{25,17},{2,10},{10... | collective-permute-start | bytes 12296 | tf_op jit(solution)/shard_map/ppermute | solution.py:42
  4.6 3.7 %collective-permute-start.1 = (f32[8,128]{1,0:T(8,128)S(1)}, f32[8,128]{1,0:T(8,128)S(1)}, u32[]{:S(2)}, u32[]{:S(2)}) collective-permute-start(f32[8,128]{1,0:T(8,128)S(1)} %shard_map.84.refs_0_), channel_id=1, source_target_pairs={{0,16},{8,24},{16,0},{24,8},{1,17},{9,25},{17,1},{25,9},{2,18},{10... | collective-permute-start | bytes 12296 | tf_op jit(solution)/shard_map/ppermute | solution.py:42
  6.2 4.5 %collective-permute-start = (f32[8,128]{1,0:T(8,128)S(1)}, f32[8,128]{1,0:T(8,128)S(1)}, u32[]{:S(2)}, u32[]{:S(2)}) collective-permute-start(f32[8,128]{1,0:T(8,128)S(1)} %shard_map.84.refs_0_), channel_id=1, source_target_pairs={{0,24},{8,16},{16,8},{24,0},{1,25},{9,17},{17,9},{25,1},{2,26},{10... | collective-permute-start | bytes 12296 | tf_op jit(solution)/shard_map/ppermute | solution.py:42
  6.2 1.0 %copy-start.2 = (f32[1,32,4096]{2,1,0:T(8,128)S(1)}, f32[1,32,4096]{2,1,0:T(8,128)}, u32[]{:S(2)}) copy-start(f32[1,32,4096]{2,1,0:T(8,128)} %param.6) | copy-start | bytes 1572868
  7.2 1.0 %copy-start.3 = (f32[1,1,32,4096]{3,2,1,0:T(8,128)S(1)}, f32[1,1,32,4096]{3,2,1,0:T(8,128)}, u32[]{:S(2)}) copy-start(f32[1,1,32,4096]{3,2,1,0:T(8,128)} %param.8) | copy-start | bytes 1572868
  8.3 2.4 %copy-start.1 = (bf16[1,1,32,4096]{3,2,1,0:T(8,128)(2,1)S(1)}, bf16[1,1,32,4096]{3,2,1,0:T(8,128)(2,1)}, u32[]{:S(2)}) copy-start(bf16[1,1,32,4096]{3,2,1,0:T(8,128)(2,1)} %param.5) | copy-start | bytes 786436
  8.3 4.2 %copy-start.5 = (f32[1,4,4096]{2,1,0:T(4,128)S(1)}, f32[1,4,4096]{2,1,0:T(4,128)}, u32[]{:S(2)}) copy-start(f32[1,4,4096]{2,1,0:T(4,128)} %param.9) | copy-start | bytes 196612
  11.1 1.4 %collective-permute-start.3 = (bf16[16,4096]{1,0:T(8,128)(2,1)S(1)}, bf16[16,4096]{1,0:T(8,128)(2,1)S(1)}, u32[]{:S(2)}, u32[]{:S(2)}) collective-permute-start(bf16[16,4096]{1,0:T(8,128)(2,1)S(1)} %get-tuple-element.21), channel_id=1, source_target_pairs={{0,1},{1,0},{2,3},{3,2},{4,5},{5,4},{6,7},{7,6},{8,9},{9,8},{10,11... | collective-permute-start | bytes 393224 | tf_op jit(solution)/shard_map/ppermute | solution.py:42
  12.6 11.9 %copy-start.4 = (bf16[1,32,4096]{2,1,0:T(8,128)(2,1)S(1)}, bf16[1,32,4096]{2,1,0:T(8,128)(2,1)}, u32[]{:S(2)}) copy-start(bf16[1,32,4096]{2,1,0:T(8,128)(2,1)} %param.7) | copy-start | bytes 786436
  12.6 7.8 %collective-permute-start.6 = (bf16[8,4096]{1,0:T(8,128)(2,1)S(1)}, bf16[8,4096]{1,0:T(8,128)(2,1)S(1)}, u32[]{:S(2)}, u32[]{:S(2)}) collective-permute-start(bf16[8,4096]{1,0:T(8,128)(2,1)S(1)} %get-tuple-element.22.own_ref), channel_id=1, source_target_pairs={{0,4},{1,5},{2,6},{3,7},{4,0},{5,1},{6,2},{7,3},{8,12},{9,13},{10,... | collective-permute-start | bytes 196616 | tf_op jit(solution)/shard_map/ppermute | solution.py:42
  15.3 6.4 %collective-permute-start.5 = (bf16[8,4096]{1,0:T(8,128)(2,1)S(1)}, bf16[8,4096]{1,0:T(8,128)(2,1)S(1)}, u32[]{:S(2)}, u32[]{:S(2)}) collective-permute-start(bf16[8,4096]{1,0:T(8,128)(2,1)S(1)} %get-tuple-element.23), channel_id=1, source_target_pairs={{0,6},{1,7},{2,4},{3,5},{4,2},{5,3},{6,0},{7,1},{8,14},{9,15},{10,... | collective-permute-start | bytes 196616 | tf_op jit(solution)/shard_map/ppermute | solution.py:42
  16.6 5.4 %collective-permute-start.4 = (bf16[8,4096]{1,0:T(8,128)(2,1)S(1)}, bf16[8,4096]{1,0:T(8,128)(2,1)S(1)}, u32[]{:S(2)}, u32[]{:S(2)}) collective-permute-start(bf16[8,4096]{1,0:T(8,128)(2,1)S(1)} %get-tuple-element.23), channel_id=1, source_target_pairs={{0,2},{1,3},{2,0},{3,1},{4,6},{5,7},{6,4},{7,5},{8,10},{9,11},{10,... | collective-permute-start | bytes 196616 | tf_op jit(solution)/shard_map/ppermute | solution.py:42
  22.2 3.9 %collective-permute-start.9 = (bf16[8,4096]{1,0:T(8,128)(2,1)S(1)}, bf16[8,4096]{1,0:T(8,128)(2,1)S(1)}, u32[]{:S(2)}, u32[]{:S(2)}) collective-permute-start(bf16[8,4096]{1,0:T(8,128)(2,1)S(1)} %get-tuple-element.24.mine_ref), channel_id=1, source_target_pairs={{0,1},{1,0},{2,3},{3,2},{4,5},{5,4},{6,7},{7,6},{8,9},{9,8},{10,11... | collective-permute-start | bytes 196616 | tf_op jit(solution)/shard_map/ppermute | solution.py:42
  22.3 4.7 %collective-permute-start.8 = (bf16[8,4096]{1,0:T(8,128)(2,1)S(1)}, bf16[8,4096]{1,0:T(8,128)(2,1)S(1)}, u32[]{:S(2)}, u32[]{:S(2)}) collective-permute-start(bf16[8,4096]{1,0:T(8,128)(2,1)S(1)} %get-tuple-element.24.mine_ref), channel_id=1, source_target_pairs={{0,3},{1,2},{2,1},{3,0},{4,7},{5,6},{6,5},{7,4},{8,11},{9,10},{10,... | collective-permute-start | bytes 196616 | tf_op jit(solution)/shard_map/ppermute | solution.py:342
  23.0 5.1 %collective-permute-start.7 = (bf16[8,4096]{1,0:T(8,128)(2,1)S(1)}, bf16[8,4096]{1,0:T(8,128)(2,1)S(1)}, u32[]{:S(2)}, u32[]{:S(2)}) collective-permute-start(bf16[8,4096]{1,0:T(8,128)(2,1)S(1)} %get-tuple-element.24.mine_ref), channel_id=1, source_target_pairs={{0,2},{1,3},{2,0},{3,1},{4,6},{5,7},{6,4},{7,5},{8,10},{9,11},{10,... | collective-permute-start | bytes 196616 | tf_op jit(solution)/shard_map/ppermute | solution.py:42
where the time goes:
time: 29.2 us; the launch traced here: 29 us
  starting transfers between devices  11.1 us (38%)
  waiting for transfers between devices  9.99 us (34%)
  Pallas kernels  4.12 us (14%)
  local copies, waits for them, and re-layouts  3.04 us (10%)
  between operations  0.74 us (3%)
    ppermute x9, starting transfers between devices, swap(): return lax.ppermute(values, axis, pairs)  10.3 us
    ppermute x9, waiting for transfers between devices, swap(): return lax.ppermute(values, axis, pairs)  9.99 us
    pallas_call x9, Pallas kernels, kernel_call(): pl.pallas_call(body, out_shape=[jax.ShapeDtypeStruct(shape, kind) for sha...  4.12 us
    unnamed x12, local copies, waits for them, and re-layouts  3.04 us
    ppermute x1, starting transfers between devices, per_device_chips(): other_cross = lax.ppermute(decoded, 'dp', cross_pairs)  0.74 us
  transfers between devices with their start and end apart: 10, of which 6 were waited for; matrix products, arithmetic and copies ran while one was open for 0% of the time, Pallas kernels for 9%

commit v1 on v0

--- a/solution.py
+++ b/solution.py
@@ -138,7 +138,7 @@
     )(*operands)
 
 
-def squares_kernel(grad_ref, out_ref):
+def squares_of(grad_ref):
     rows, width = grad_ref.shape
     total = [jnp.zeros((LANE_ROWS, LANES), jnp.float32) for _ in range(4)]
     turn = 0
@@ -147,13 +147,34 @@
             piece = grad_ref[row : row + LANE_ROWS, column : column + LANES].astype(jnp.float32)
             total[turn % 4] = total[turn % 4] + piece * piece
             turn += 1
-    out_ref[...] = (total[0] + total[1]) + (total[2] + total[3])
-
-
-def base_kernel(momentum_ref, error_ref, base_ref):
-    for row in range(0, base_ref.shape[0], LANE_ROWS):
-        rows = slice(row, row + LANE_ROWS)
-        base_ref[rows, :] = beta_one * momentum_ref[rows, :] + error_ref[rows, :]
+    return (total[0] + total[1]) + (total[2] + total[3])
+
+
+def squares_kernel(grad_ref, out_ref):
+    out_ref[...] = squares_of(grad_ref)
+
+
+def both_squares_kernel(own_ref, other_grad_ref, out_ref):
+    out_ref[:LANE_ROWS, :] = own_ref[...]
+    out_ref[LANE_ROWS:, :] = squares_of(other_grad_ref)
+
+
+def base_rows(momentum_ref, error_ref, rows):
+    return beta_one * momentum_ref[rows, :] + error_ref[rows, :]
+
+
+def prepare_kernel(chip_rows, momentum_ref, error_ref, other_error_ref, grad_ref, other_grad_ref, base_ref, *outs):
+    chip, first = position()
+    for turn in range(2):
+        parity = (chip + turn) % 2
+        block = slice(turn * chip_rows, (turn + 1) * chip_rows)
+        low, high = (chip_rows_at(place, chip_rows) for place in (parity, parity + 2))
+        for errors, grads, base_out, grad_out in ((error_ref, grad_ref, *outs[:2]), (other_error_ref, other_grad_ref, *outs[2:])):
+            halves = [base_rows(momentum_ref, errors, rows) for rows in (low, high)]
+            if errors is error_ref:
+                base_ref[low, :], base_ref[high, :] = halves
+            base_out[block, :] = pick_half(*halves, first)
+            grad_out[block, :] = pick_half(*(grads[rows, :].astype(jnp.float32) for rows in (low, high)), first)
 
 
 def row_scale_of(values):
@@ -182,53 +203,45 @@
     )
 
 
-def worker_kernel(experts, chip_rows, *refs):
+def worker_kernel(replicas, experts, entries, chip_rows, *refs):
     parts = refs[:experts]
-    grad_ref, base_ref, same_ref, cross_ref, send_ref, scale_ref, sum_ref = refs[experts:]
+    base_ref, grad_ref, other_base_ref, other_grad_ref, error_ref, same_ref, cross_ref, gain_ref = refs[experts:]
     total = parts[0][...]
     for part in parts[1:]:
         total = total + part[...]
-    count = experts * grad_ref.shape[0] * grad_ref.shape[1]
-    squares = jnp.sum(total, axis=(0, 1), keepdims=True)
-    factor = jnp.minimum(1.0, rms_limit / jnp.sqrt(squares / count + 1e-06))
-    chip, first = position()
-    for turn, mine_ref in enumerate((same_ref, cross_ref)):
-        parity = (chip + turn) % 2
-        decoded = []
-        for block in (parity, parity + 2):
-            rows = chip_rows_at(block, chip_rows)
-            values = base_ref[rows, :] + (1.0 - beta_one) * (grad_ref[rows, :].astype(jnp.float32) * factor)
-            sum_ref[rows, :] = values
-            scale = row_scale_of(values)
-            scale_ref[rows, :] = jnp.broadcast_to(scale, (chip_rows, LANES))
-            decoded.append(coded(values, scale))
-        mine_ref[...] = pick_half(*decoded, first)
-        send_ref[turn * chip_rows : (turn + 1) * chip_rows, :] = pick_half(*decoded, jnp.logical_not(first)).astype(
-            jnp.bfloat16
-        )
-
-
-def worker_error_kernel(chip_rows, scale_ref, sum_ref, variance_ref, new_hbm, inverse_ref, new_ref, sems):
+    gains = []
+    for row in (0, LANE_ROWS):
+        squares = jnp.sum(total[row : row + LANE_ROWS], axis=(0, 1), keepdims=True)
+        factor = jnp.minimum(1.0, rms_limit / jnp.sqrt(squares / (experts * entries) + 1e-06))
+        gains.append((1.0 - beta_one) * factor)
+    gain_ref[...] = jnp.broadcast_to(gains[0], gain_ref.shape)
+    chip, _ = position()
+    error = replicas * error_ref[...]
+    none = jnp.zeros_like(error)
+    owned = jnp.where(chip < 2, jnp.concatenate([error, none]), jnp.concatenate([none, error]))
+    for turn, out_ref in enumerate((same_ref, cross_ref)):
+        block = slice(turn * chip_rows, (turn + 1) * chip_rows)
+        values = base_ref[block, :] + gains[0] * grad_ref[block, :]
+        other = other_base_ref[block, :] + gains[1] * other_grad_ref[block, :]
+        total = coded(values, row_scale_of(values)) + coded(other, row_scale_of(other))
+        if turn == 0:
+            total = total + owned
+        out_ref[...] = total.astype(jnp.bfloat16)
+
+
+def worker_error_kernel(chip_rows, gain_ref, grad_ref, base_ref, variance_ref, new_hbm, inverse_ref, new_ref, sems):
+    gain = gain_ref[0:1, 0:1]
     copies = []
-    chunks = [slice(row, row + chip_rows) for row in range(0, sum_ref.shape[0], chip_rows)]
+    chunks = [slice(row, row + chip_rows) for row in range(0, base_ref.shape[0], chip_rows)]
     for i, rows in enumerate(chunks):
-        values = sum_ref[rows, :]
-        new_ref[rows, :] = values - coded(values, scale_ref[rows, 0:1])
+        values = base_ref[rows, :] + gain * grad_ref[rows, :].astype(jnp.float32)
+        new_ref[rows, :] = values - coded(values, row_scale_of(values))
         copies.append(pltpu.make_async_copy(new_ref.at[rows, :], new_hbm.at[rows, :], sems.at[i]))
         copies[-1].start()
     for rows in chunks:
         inverse_ref[rows, :] = 1.0 / (jnp.sqrt(variance_ref[rows, :].astype(jnp.float32)) + adam_eps)
     for copy in copies:
         copy.wait()
-
-
-def chip_sum_kernel(replicas, chip_rows, same_ref, cross_ref, got_ref, error_ref, same_out, cross_out):
-    chip, _ = position()
-    error = replicas * error_ref[...]
-    none = jnp.zeros_like(error)
-    owned = jnp.where(chip < 2, jnp.concatenate([error, none]), jnp.concatenate([none, error]))
-    same_out[...] = (same_ref[...] + got_ref[:chip_rows, :].astype(jnp.float32) + owned).astype(jnp.bfloat16)
-    cross_out[...] = (cross_ref[...] + got_ref[chip_rows:, :].astype(jnp.float32)).astype(jnp.bfloat16)
 
 
 def owner_kernel(replicas, own_ref, near_ref, far_ref, across_ref, sum_ref, out_ref):
@@ -304,21 +317,25 @@
     def core_swap(values):
         return swap(values, "dp", 1, 1, CORES, replicas)
 
-    (part,) = kernel_call(squares_kernel, [((LANE_ROWS, LANES), f32)], [grad], flops=2 * rows * width)
+    other_grad = core_swap(grad)
+    other_error = core_swap(error)
+    (own_part,) = kernel_call(squares_kernel, [((LANE_ROWS, LANES), f32)], [grad], flops=10**9)
+    (part,) = kernel_call(
+        both_squares_kernel, [((CORES * LANE_ROWS, LANES), f32)], [own_part, other_grad], flops=2 * rows * width
+    )
     parts = [part] + [swap(part, "expert", step, 1, experts, experts) for step in reversed(range(1, experts))]
-    (base,) = kernel_call(base_kernel, [((rows, width), f32)], [moment, error], flops=2 * rows * width)
-    same, cross, send, scales, sums = kernel_call(
-        functools.partial(worker_kernel, experts, chip_rows),
-        [(block, f32), (block, f32), ((2 * chip_rows, width), bf16), ((rows, LANES), f32), ((rows, width), f32)],
-        parts + [grad, base],
+    pair = (2 * chip_rows, width)
+    base, *halves = kernel_call(
+        functools.partial(prepare_kernel, chip_rows),
+        [((rows, width), f32)] + [(pair, f32)] * 4,
+        [moment, error, other_error, grad, other_grad],
+        flops=4 * rows * width,
+    )
+    same_sum, cross_sum, gain = kernel_call(
+        functools.partial(worker_kernel, replicas, experts, rows * width, chip_rows),
+        [(block, bf16), (block, bf16), ((LANE_ROWS, LANES), f32)],
+        [*parts, *halves, server_error[0]],
         flops=20 * rows * width,
-    )
-    got = core_swap(send)
-    same_sum, cross_sum = kernel_call(
-        functools.partial(chip_sum_kernel, replicas, chip_rows),
-        [(block, bf16), (block, bf16)],
-        [same, cross, got, server_error[0]],
-        flops=4 * rows * width,
     )
     far = chip_swap(cross_sum, 3)
     across = chip_swap(same_sum, 2)
@@ -326,7 +343,7 @@
     worker_new, inverse = kernel_call(
         functools.partial(worker_error_kernel, chip_rows),
         [((rows, width), f32), ((rows, width), f32)],
-        [scales, sums, variance[0]],
+        [gain, grad, base, variance[0]],
         out_space=[pltpu.HBM, pltpu.VMEM],
         scratch=[pltpu.VMEM((rows, width), f32), pltpu.SemaphoreType.DMA((chips,))],
         flops=20 * rows * width,

time: 29.2 us -> 28.8 us (0.986)
  local copies, waits for them, and re-layouts: 3.04 us -> 0.98 us
  waiting for transfers between devices: 9.99 us -> 11 us
  starting transfers between devices: 11.1 us -> 11.5 us
    unnamed x12, local copies, waits for them, and re-layouts: 3.04 us -> 0.98 us
    ppermute x9 -> x10, starting transfers between devices: 10.3 us -> 11.4 us  [swap(): return lax.ppermute(values, axis, pairs)]
    ppermute x9 -> x10, waiting for transfers between devices: 9.99 us -> 11 us  [swap(): return lax.ppermute(values, axis, pairs)]
    ppermute x1, starting transfers between devices: 0.74 us -> 0.1 us  [per_device_chips(): other_cross = lax.ppermute(decoded, 'dp', cross_pairs)]
  transfers between devices with their start and end apart: 10 -> 11, of which waited for: 6 -> 7; matrix products, arithmetic and copies ran while one was open for 0% -> 0% of each run, Pallas kernels for 9% -> 11%
where the time goes in v1:
time: 28.8 us; the launch traced here: 28.7 us
  starting transfers between devices  11.5 us (40%)
  waiting for transfers between devices  11 us (38%)
  Pallas kernels  4.41 us (15%)
  local copies, waits for them, and re-layouts  0.98 us (3%)
  between operations  0.74 us (3%)
    ppermute x10, starting transfers between devices, swap(): return lax.ppermute(values, axis, pairs)  11.4 us
    ppermute x10, waiting for transfers between devices, swap(): return lax.ppermute(values, axis, pairs)  11 us
    pallas_call x9, Pallas kernels, kernel_call(): pl.pallas_call(body, out_shape=[jax.ShapeDtypeStruct(shape, kind) for sha...  4.41 us
    unnamed x12, local copies, waits for them, and re-layouts  0.98 us
  transfers between devices with their start and end apart: 11, of which 7 were waited for; matrix products, arithmetic and copies ran while one was open for 0% of the time, Pallas kernels for 11%

profile of v1, /device:TPU:0, one launch (start us, length us, event | category | flops | bytes accessed | tf_op | source)
XLA Modules:
  0.0 28.7 jit_solution(10500518405298851371)
XLA Ops:
  0.6 0.6 %collective-permute-start.4 = (f32[32,4096]{1,0:T(8,128)}, f32[32,4096]{1,0:T(8,128)S(1)}, u32[]{:S(2)}, u32[]{:S(2)}) collective-permute-start(f32[32,4096]{1,0:T(8,128)} %bitcast.14), channel_id=1, source_target_pairs={{0,1},{1,0},{2,3},{3,2},{4,5},{5,4},{6,7},{7,6},{8,9},{9,8},{10,11... | collective-permute-start | bytes 1572872 | tf_op jit(solution)/shard_map/ppermute | solution.py:42
  1.2 0.1 collective-permute-start
  1.3 0.0 copy-start
  1.3 0.9 %copy-done = bf16[1,1,32,4096]{3,2,1,0:T(8,128)(2,1)S(1)} copy-done((bf16[1,1,32,4096]{3,2,1,0:T(8,128)(2,1)S(1)}, bf16[1,1,32,4096]{3,2,1,0:T(8,128)(2,1)}, u32[]{:S(2)}) %copy-start) | copy-done | bytes 262168
  2.2 0.0 copy-start.2
  2.2 0.0 copy-start.3
  2.2 0.0 copy-start.1
  2.3 1.1 %collective-permute-done.other_grad_ref = bf16[32,4096]{1,0:T(8,128)(2,1)S(1)} collective-permute-done((bf16[32,4096]{1,0:T(8,128)(2,1)}, bf16[32,4096]{1,0:T(8,128)(2,1)S(1)}, u32[]{:S(2)}, u32[]{:S(2)}) %collective-permute-start) | collective-permute-done | bytes 262176 | tf_op jit(solution)/shard_map/ppermute | solution.py:42
  3.3 2.9 %collective-permute-start.3 = (f32[16,128]{1,0:T(8,128)S(1)}, f32[16,128]{1,0:T(8,128)S(1)}, u32[]{:S(2)}, u32[]{:S(2)}) collective-permute-start(f32[16,128]{1,0:T(8,128)S(1)} %shard_map.85.refs_0_), channel_id=1, source_target_pairs={{0,8},{8,0},{16,24},{24,16},{1,9},{9,1},{17,25},{25,17},{2,10},{10... | collective-permute-start | bytes 24584 | tf_op jit(solution)/shard_map/ppermute | solution.py:42
  6.3 1.5 %collective-permute-start.2 = (f32[16,128]{1,0:T(8,128)S(1)}, f32[16,128]{1,0:T(8,128)S(1)}, u32[]{:S(2)}, u32[]{:S(2)}) collective-permute-start(f32[16,128]{1,0:T(8,128)S(1)} %shard_map.85.refs_0_), channel_id=1, source_target_pairs={{0,16},{8,24},{16,0},{24,8},{1,17},{9,25},{17,1},{25,9},{2,18},{10... | collective-permute-start | bytes 24584 | tf_op jit(solution)/shard_map/ppermute | solution.py:42
  7.8 0.0 collective-permute-start.1
  7.8 0.0 collective-permute-done.4.other_error_ref
  7.8 0.0 copy-done.2
  7.8 0.0 copy-done.3
  7.8 0.0 copy-done.1
  7.8 0.0 copy-start.5
  7.8 0.3 %shard_map.86 = (f32[32,4096]{1,0:T(8,128)S(1)}, f32[16,4096]{1,0:T(8,128)S(1)}, f32[16,4096]{1,0:T(8,128)S(1)}, f32[16,4096]{1,0:T(8,128)S(1)}, f32[16,4096]{1,0:T(8,128)S(1)}) custom-call(f32[32,4096]{1,0:T(8,128)S(1)} %bitcast.13, f32[32,4096]{1,0:T(8,128)S(1)} %bitcast.15, f32[32,4096]{1,0:T(8,128)S(1)} %collective-permute-done.4.other_error_ref, ...), custom_call_target="tpu_custom_call" | custom-call | flops 524288 | bytes 3670016 | tf_op jit(solution)/shard_map/pallas_call | solution.py:129
  8.2 0.0 collective-permute-done.3.refs_3_
  8.2 1.7 %collective-permute-done.2.refs_2_ = f32[16,128]{1,0:T(8,128)S(1)} collective-permute-done((f32[16,128]{1,0:T(8,128)S(1)}, f32[16,128]{1,0:T(8,128)S(1)}, u32[]{:S(2)}, u32[]{:S(2)}) %collective-permute-start.2) | collective-permute-done | bytes 8224 | tf_op jit(solution)/shard_map/ppermute | solution.py:42
  9.9 2.4 %collective-permute-done.1.refs_1_ = f32[16,128]{1,0:T(8,128)S(1)} collective-permute-done((f32[16,128]{1,0:T(8,128)S(1)}, f32[16,128]{1,0:T(8,128)S(1)}, u32[]{:S(2)}, u32[]{:S(2)}) %collective-permute-start.1) | collective-permute-done | bytes 8224 | tf_op jit(solution)/shard_map/ppermute | solution.py:42
  12.3 0.0 copy-done.5
  12.3 0.4 %shard_map.87 = (bf16[8,4096]{1,0:T(8,128)(2,1)S(1)}, bf16[8,4096]{1,0:T(8,128)(2,1)S(1)}, f32[8,128]{1,0:T(8,128)S(1)}) custom-call(f32[16,128]{1,0:T(8,128)S(1)} %shard_map.85.refs_0_, f32[16,128]{1,0:T(8,128)S(1)} %collective-permute-done.1.refs_1_, f32[16,128]{1,0:T(8,128)S(1)} %collective-permute-done.2.refs_2_, ...), custom_call_target="tpu_custom_call" | custom-call | flops 2621440 | bytes 1282048 | tf_op jit(solution)/shard_map/pallas_call | solution.py:129
  12.7 0.0 copy-start.4
  12.7 2.7 %collective-permute-start.7 = (bf16[8,4096]{1,0:T(8,128)(2,1)S(1)}, bf16[8,4096]{1,0:T(8,128)(2,1)S(1)}, u32[]{:S(2)}, u32[]{:S(2)}) collective-permute-start(bf16[8,4096]{1,0:T(8,128)(2,1)S(1)} %get-tuple-element.24.own_ref), channel_id=1, source_target_pairs={{0,4},{1,5},{2,6},{3,7},{4,0},{5,1},{6,2},{7,3},{8,12},{9,13},{10,... | collective-permute-start | bytes 196616 | tf_op jit(solution)/shard_map/ppermute | solution.py:42
  15.4 1.3 %collective-permute-start.6 = (bf16[8,4096]{1,0:T(8,128)(2,1)S(1)}, bf16[8,4096]{1,0:T(8,128)(2,1)S(1)}, u32[]{:S(2)}, u32[]{:S(2)}) collective-permute-start(bf16[8,4096]{1,0:T(8,128)(2,1)S(1)} %get-tuple-element.25), channel_id=1, source_target_pairs={{0,6},{1,7},{2,4},{3,5},{4,2},{5,3},{6,0},{7,1},{8,14},{9,15},{10,... | collective-permute-start | bytes 196616 | tf_op jit(solution)/shard_map/ppermute | solution.py:42
  16.7 0.2 collective-permute-start.5
  17.0 3.0 %collective-permute-done.7.across_ref = bf16[8,4096]{1,0:T(8,128)(2,1)S(1)} collective-permute-done((bf16[8,4096]{1,0:T(8,128)(2,1)S(1)}, bf16[8,4096]{1,0:T(8,128)(2,1)S(1)}, u32[]{:S(2)}, u32[]{:S(2)}) %collective-permute-start.7) | collective-permute-done | bytes 65568 | tf_op jit(solution)/shard_map/ppermute | solution.py:42
  19.9 1.6 %collective-permute-done.6.far_ref = bf16[8,4096]{1,0:T(8,128)(2,1)S(1)} collective-permute-done((bf16[8,4096]{1,0:T(8,128)(2,1)S(1)}, bf16[8,4096]{1,0:T(8,128)(2,1)S(1)}, u32[]{:S(2)}, u32[]{:S(2)}) %collective-permute-start.6) | collective-permute-done | bytes 65568 | tf_op jit(solution)/shard_map/ppermute | solution.py:42
  21.6 0.2 collective-permute-done.5.near_ref
  21.7 0.2 shard_map.88
  21.9 0.1 collective-permute-start.10
  22.0 0.1 collective-permute-start.9
  22.1 2.0 %collective-permute-start.8 = (bf16[8,4096]{1,0:T(8,128)(2,1)S(1)}, bf16[8,4096]{1,0:T(8,128)(2,1)S(1)}, u32[]{:S(2)}, u32[]{:S(2)}) collective-permute-start(bf16[8,4096]{1,0:T(8,128)(2,1)S(1)} %get-tuple-element.26.mine_ref), channel_id=1, source_target_pairs={{0,2},{1,3},{2,0},{3,1},{4,6},{5,7},{6,4},{7,5},{8,10},{9,11},{10,... | collective-permute-start | bytes 196616 | tf_op jit(solution)/shard_map/ppermute | solution.py:42
  24.1 0.0 copy-done.4
  24.1 1.0 %shard_map.89 = (f32[32,4096]{1,0:T(8,128)}, f32[32,4096]{1,0:T(8,128)S(1)}) custom-call(f32[8,128]{1,0:T(8,128)S(1)} %get-tuple-element.27.gain_ref, bf16[32,4096]{1,0:T(8,128)(2,1)S(1)} %bitcast.12, f32[32,4096]{1,0:T(8,128)S(1)} %get-tuple-element.28.base_ref, bf16[32,4096]{1,0:T(8,128)(2,1)S(1)} %bitcast.16), custom_call_target="tpu_custom_call" | custom-call | flops 2621440 | bytes 2101248 | tf_op jit(solution)/shard_map/pallas_call | solution.py:129
  25.2 0.8 %shard_map.92 = f32[4,4096]{1,0:T(4,128)} custom-call(f32[8,4096]{1,0:T(8,128)S(1)} %get-tuple-element.35.sum_ref), custom_call_target="tpu_custom_call" | custom-call | flops 655360 | bytes 196608 | tf_op jit(solution)/shard_map/pallas_call | solution.py:129
  25.9 0.0 collective-permute-done.10.other_ref
  25.9 0.8 %shard_map.90 = (f32[32,4096]{1,0:T(8,128)}, bf16[32,4096]{1,0:T(8,128)(2,1)}) custom-call(bf16[8,4096]{1,0:T(8,128)(2,1)S(1)} %get-tuple-element.26.mine_ref, bf16[8,4096]{1,0:T(8,128)(2,1)S(1)} %collective-permute-done.10.other_ref, f32[32,4096]{1,0:T(8,128)S(1)} %get-tuple-element.29.inverse_ref), custom_call_target="tpu_custom_call" | custom-call | flops 262144 | bytes 1441792 | tf_op jit(solution)/shard_map/pallas_call | solution.py:129
  26.8 0.0 collective-permute-done.9.other_ref
  26.8 1.1 %collective-permute-done.8.mine_ref = bf16[8,4096]{1,0:T(8,128)(2,1)S(1)} collective-permute-done((bf16[8,4096]{1,0:T(8,128)(2,1)S(1)}, bf16[8,4096]{1,0:T(8,128)(2,1)S(1)}, u32[]{:S(2)}, u32[]{:S(2)}) %collective-permute-start.8) | collective-permute-done | bytes 65568 | tf_op jit(solution)/shard_map/ppermute | solution.py:42
  27.8 0.8 %shard_map.91 = (f32[32,4096]{1,0:T(8,128)}, bf16[32,4096]{1,0:T(8,128)(2,1)}) custom-call(bf16[8,4096]{1,0:T(8,128)(2,1)S(1)} %collective-permute-done.8.mine_ref, bf16[8,4096]{1,0:T(8,128)(2,1)S(1)} %collective-permute-done.9.other_ref, f32[32,4096]{1,0:T(8,128)S(1)} %get-tuple-element.29.inverse_ref, ...), custom_call_target="tpu_custom_call", output_to_operand_aliasing={{0}: (3, {}), {1}: (4, {})} | custom-call | flops 262144 | bytes 2228224 | tf_op jit(solution)/shard_map/pallas_call | solution.py:129
  (2 shorter events, 0.0 us)
Async XLA Ops:
  0.6 7.2 %collective-permute-start.4 = (f32[32,4096]{1,0:T(8,128)}, f32[32,4096]{1,0:T(8,128)S(1)}, u32[]{:S(2)}, u32[]{:S(2)}) collective-permute-start(f32[32,4096]{1,0:T(8,128)} %bitcast.14), channel_id=1, source_target_pairs={{0,1},{1,0},{2,3},{3,2},{4,5},{5,4},{6,7},{7,6},{8,9},{9,8},{10,11... | collective-permute-start | bytes 1572872 | tf_op jit(solution)/shard_map/ppermute | solution.py:42
  1.2 2.1 %collective-permute-start = (bf16[32,4096]{1,0:T(8,128)(2,1)}, bf16[32,4096]{1,0:T(8,128)(2,1)S(1)}, u32[]{:S(2)}, u32[]{:S(2)}) collective-permute-start(bf16[32,4096]{1,0:T(8,128)(2,1)} %bitcast.9), channel_id=1, source_target_pairs={{0,1},{1,0},{2,3},{3,2},{4,5},{5,4},{6,7},{7,6},{8,9},{9,8},{10,11... | collective-permute-start | bytes 786440 | tf_op jit(solution)/shard_map/ppermute | solution.py:42
  1.3 0.9 %copy-start = (bf16[1,1,32,4096]{3,2,1,0:T(8,128)(2,1)S(1)}, bf16[1,1,32,4096]{3,2,1,0:T(8,128)(2,1)}, u32[]{:S(2)}) copy-start(bf16[1,1,32,4096]{3,2,1,0:T(8,128)(2,1)} %param.5) | copy-start | bytes 786436
  2.2 5.6 %copy-start.2 = (f32[1,32,4096]{2,1,0:T(8,128)S(1)}, f32[1,32,4096]{2,1,0:T(8,128)}, u32[]{:S(2)}) copy-start(f32[1,32,4096]{2,1,0:T(8,128)} %param.6) | copy-start | bytes 1572868
  2.2 5.6 %copy-start.3 = (f32[1,1,32,4096]{3,2,1,0:T(8,128)S(1)}, f32[1,1,32,4096]{3,2,1,0:T(8,128)}, u32[]{:S(2)}) copy-start(f32[1,1,32,4096]{3,2,1,0:T(8,128)} %param.8) | copy-start | bytes 1572868
  2.2 5.6 %copy-start.1 = (bf16[1,1,32,4096]{3,2,1,0:T(8,128)(2,1)S(1)}, bf16[1,1,32,4096]{3,2,1,0:T(8,128)(2,1)}, u32[]{:S(2)}) copy-start(bf16[1,1,32,4096]{3,2,1,0:T(8,128)(2,1)} %param.5) | copy-start | bytes 786436
  3.3 4.8 %collective-permute-start.3 = (f32[16,128]{1,0:T(8,128)S(1)}, f32[16,128]{1,0:T(8,128)S(1)}, u32[]{:S(2)}, u32[]{:S(2)}) collective-permute-start(f32[16,128]{1,0:T(8,128)S(1)} %shard_map.85.refs_0_), channel_id=1, source_target_pairs={{0,8},{8,0},{16,24},{24,16},{1,9},{9,1},{17,25},{25,17},{2,10},{10... | collective-permute-start | bytes 24584 | tf_op jit(solution)/shard_map/ppermute | solution.py:42
  6.3 3.7 %collective-permute-start.2 = (f32[16,128]{1,0:T(8,128)S(1)}, f32[16,128]{1,0:T(8,128)S(1)}, u32[]{:S(2)}, u32[]{:S(2)}) collective-permute-start(f32[16,128]{1,0:T(8,128)S(1)} %shard_map.85.refs_0_), channel_id=1, source_target_pairs={{0,16},{8,24},{16,0},{24,8},{1,17},{9,25},{17,1},{25,9},{2,18},{10... | collective-permute-start | bytes 24584 | tf_op jit(solution)/shard_map/ppermute | solution.py:42
  7.8 4.5 %collective-permute-start.1 = (f32[16,128]{1,0:T(8,128)S(1)}, f32[16,128]{1,0:T(8,128)S(1)}, u32[]{:S(2)}, u32[]{:S(2)}) collective-permute-start(f32[16,128]{1,0:T(8,128)S(1)} %shard_map.85.refs_0_), channel_id=1, source_target_pairs={{0,24},{8,16},{16,8},{24,0},{1,25},{9,17},{17,9},{25,1},{2,26},{10... | collective-permute-start | bytes 24584 | tf_op jit(solution)/shard_map/ppermute | solution.py:42
  7.8 4.5 %copy-start.5 = (f32[1,4,4096]{2,1,0:T(4,128)S(1)}, f32[1,4,4096]{2,1,0:T(4,128)}, u32[]{:S(2)}) copy-start(f32[1,4,4096]{2,1,0:T(4,128)} %param.9) | copy-start | bytes 196612
  12.7 11.4 %copy-start.4 = (bf16[1,32,4096]{2,1,0:T(8,128)(2,1)S(1)}, bf16[1,32,4096]{2,1,0:T(8,128)(2,1)}, u32[]{:S(2)}) copy-start(bf16[1,32,4096]{2,1,0:T(8,128)(2,1)} %param.7) | copy-start | bytes 786436
  12.7 7.2 %collective-permute-start.7 = (bf16[8,4096]{1,0:T(8,128)(2,1)S(1)}, bf16[8,4096]{1,0:T(8,128)(2,1)S(1)}, u32[]{:S(2)}, u32[]{:S(2)}) collective-permute-start(bf16[8,4096]{1,0:T(8,128)(2,1)S(1)} %get-tuple-element.24.own_ref), channel_id=1, source_target_pairs={{0,4},{1,5},{2,6},{3,7},{4,0},{5,1},{6,2},{7,3},{8,12},{9,13},{10,... | collective-permute-start | bytes 196616 | tf_op jit(solution)/shard_map/ppermute | solution.py:42
  15.4 6.2 %collective-permute-start.6 = (bf16[8,4096]{1,0:T(8,128)(2,1)S(1)}, bf16[8,4096]{1,0:T(8,128)(2,1)S(1)}, u32[]{:S(2)}, u32[]{:S(2)}) collective-permute-start(bf16[8,4096]{1,0:T(8,128)(2,1)S(1)} %get-tuple-element.25), channel_id=1, source_target_pairs={{0,6},{1,7},{2,4},{3,5},{4,2},{5,3},{6,0},{7,1},{8,14},{9,15},{10,... | collective-permute-start | bytes 196616 | tf_op jit(solution)/shard_map/ppermute | solution.py:42
  16.7 5.0 %collective-permute-start.5 = (bf16[8,4096]{1,0:T(8,128)(2,1)S(1)}, bf16[8,4096]{1,0:T(8,128)(2,1)S(1)}, u32[]{:S(2)}, u32[]{:S(2)}) collective-permute-start(bf16[8,4096]{1,0:T(8,128)(2,1)S(1)} %get-tuple-element.25), channel_id=1, source_target_pairs={{0,2},{1,3},{2,0},{3,1},{4,6},{5,7},{6,4},{7,5},{8,10},{9,11},{10,... | collective-permute-start | bytes 196616 | tf_op jit(solution)/shard_map/ppermute | solution.py:42
  21.9 4.0 %collective-permute-start.10 = (bf16[8,4096]{1,0:T(8,128)(2,1)S(1)}, bf16[8,4096]{1,0:T(8,128)(2,1)S(1)}, u32[]{:S(2)}, u32[]{:S(2)}) collective-permute-start(bf16[8,4096]{1,0:T(8,128)(2,1)S(1)} %get-tuple-element.26.mine_ref), channel_id=1, source_target_pairs={{0,1},{1,0},{2,3},{3,2},{4,5},{5,4},{6,7},{7,6},{8,9},{9,8},{10,11... | collective-permute-start | bytes 196616 | tf_op jit(solution)/shard_map/ppermute | solution.py:42
  22.0 4.8 %collective-permute-start.9 = (bf16[8,4096]{1,0:T(8,128)(2,1)S(1)}, bf16[8,4096]{1,0:T(8,128)(2,1)S(1)}, u32[]{:S(2)}, u32[]{:S(2)}) collective-permute-start(bf16[8,4096]{1,0:T(8,128)(2,1)S(1)} %get-tuple-element.26.mine_ref), channel_id=1, source_target_pairs={{0,3},{1,2},{2,1},{3,0},{4,7},{5,6},{6,5},{7,4},{8,11},{9,10},{10,... | collective-permute-start | bytes 196616 | tf_op jit(solution)/shard_map/ppermute | solution.py:359
  22.1 5.8 %collective-permute-start.8 = (bf16[8,4096]{1,0:T(8,128)(2,1)S(1)}, bf16[8,4096]{1,0:T(8,128)(2,1)S(1)}, u32[]{:S(2)}, u32[]{:S(2)}) collective-permute-start(bf16[8,4096]{1,0:T(8,128)(2,1)S(1)} %get-tuple-element.26.mine_ref), channel_id=1, source_target_pairs={{0,2},{1,3},{2,0},{3,1},{4,6},{5,7},{6,4},{7,5},{8,10},{9,11},{10,... | collective-permute-start | bytes 196616 | tf_op jit(solution)/shard_map/ppermute | solution.py:42

commit v2 on v1

--- a/solution.py
+++ b/solution.py
@@ -206,9 +206,9 @@
 def worker_kernel(replicas, experts, entries, chip_rows, *refs):
     parts = refs[:experts]
     base_ref, grad_ref, other_base_ref, other_grad_ref, error_ref, same_ref, cross_ref, gain_ref = refs[experts:]
-    total = parts[0][...]
-    for part in parts[1:]:
-        total = total + part[...]
+    own, near, heard, other_heard = (part[...] for part in parts)
+    other_heard = jnp.concatenate([other_heard[LANE_ROWS:], other_heard[:LANE_ROWS]])
+    total = (own + near) + (heard + other_heard)
     gains = []
     for row in (0, LANE_ROWS):
         squares = jnp.sum(total[row : row + LANE_ROWS], axis=(0, 1), keepdims=True)
@@ -323,7 +323,15 @@
     (part,) = kernel_call(
         both_squares_kernel, [((CORES * LANE_ROWS, LANES), f32)], [own_part, other_grad], flops=2 * rows * width
     )
-    parts = [part] + [swap(part, "expert", step, 1, experts, experts) for step in reversed(range(1, experts))]
+    split_pairs = [
+        (expert * replicas + place, (expert ^ (2 if place % CORES == 0 else 3)) * replicas + place)
+        for expert in range(experts)
+        for place in range(replicas)
+    ]
+    heard = lax.ppermute(part, ("expert", "dp"), split_pairs)
+    near_part = swap(part, "expert", 1, 1, experts, experts)
+    other_heard = core_swap(heard)
+    parts = [part, near_part, heard, other_heard]
     pair = (2 * chip_rows, width)
     base, *halves = kernel_call(
         functools.partial(prepare_kernel, chip_rows),
@@ -365,7 +373,7 @@
 
 
 def solution(mesh):
-    if mesh.shape["dp"] == 4 * CORES:
+    if mesh.shape["dp"] == 4 * CORES and mesh.shape["expert"] == 4:
         return placed_step(mesh, per_device_chips)
     return placed_step(mesh, per_device)
 

time: 28.8 us -> 26.5 us (0.920)
  waiting for transfers between devices: 11 us -> 8.5 us
    ppermute x10 -> x9, starting transfers between devices: 11.4 us -> 7.76 us  [swap(): return lax.ppermute(values, axis, pairs)]
    ppermute x0 -> x1, starting transfers between devices: none -> 2.94 us  [per_device_chips(): heard = lax.ppermute(part, ('expert', 'dp'), split_pairs)]
    ppermute x10 -> x9, waiting for transfers between devices: 11 us -> 8.36 us  [swap(): return lax.ppermute(values, axis, pairs)]
    ppermute x1, starting transfers between devices: 0.1 us -> 1 us  [per_device_chips(): other_cross = lax.ppermute(decoded, 'dp', cross_pairs)]
where the time goes in v2:
time: 26.5 us; the launch traced here: 26.3 us
  starting transfers between devices  11.7 us (44%)
  waiting for transfers between devices  8.5 us (32%)
  Pallas kernels  4.41 us (17%)
  local copies, waits for them, and re-layouts  0.98 us (4%)
  between operations  0.73 us (3%)
    ppermute x9, waiting for transfers between devices, swap(): return lax.ppermute(values, axis, pairs)  8.36 us
    ppermute x9, starting transfers between devices, swap(): return lax.ppermute(values, axis, pairs)  7.76 us
    pallas_call x9, Pallas kernels, kernel_call(): pl.pallas_call(body, out_shape=[jax.ShapeDtypeStruct(shape, kind) for sha...  4.41 us
    ppermute x1, starting transfers between devices, per_device_chips(): heard = lax.ppermute(part, ('expert', 'dp'), split_pairs)  2.94 us
    ppermute x1, starting transfers between devices, per_device_chips(): other_cross = lax.ppermute(decoded, 'dp', cross_pairs)  1 us
    unnamed x12, local copies, waits for them, and re-layouts  0.98 us
  transfers between devices with their start and end apart: 11, of which 7 were waited for; matrix products, arithmetic and copies ran while one was open for 0% of the time, Pallas kernels for 11%

profile of v2, /device:TPU:0, one launch (start us, length us, event | category | flops | bytes accessed | tf_op | source)
XLA Modules:
  0.0 26.3 jit_solution(692558657125260092)
XLA Ops:
  0.6 0.6 %collective-permute-start.4 = (f32[32,4096]{1,0:T(8,128)}, f32[32,4096]{1,0:T(8,128)S(1)}, u32[]{:S(2)}, u32[]{:S(2)}) collective-permute-start(f32[32,4096]{1,0:T(8,128)} %bitcast.14), channel_id=1, source_target_pairs={{0,1},{1,0},{2,3},{3,2},{4,5},{5,4},{6,7},{7,6},{8,9},{9,8},{10,11... | collective-permute-start | bytes 1572872 | tf_op jit(solution)/shard_map/ppermute | solution.py:42
  1.2 0.1 collective-permute-start
  1.3 0.0 copy-start
  1.3 0.9 %copy-done = bf16[1,1,32,4096]{3,2,1,0:T(8,128)(2,1)S(1)} copy-done((bf16[1,1,32,4096]{3,2,1,0:T(8,128)(2,1)S(1)}, bf16[1,1,32,4096]{3,2,1,0:T(8,128)(2,1)}, u32[]{:S(2)}) %copy-start) | copy-done | bytes 262168
  2.2 0.0 copy-start.2
  2.2 0.0 copy-start.3
  2.2 0.0 copy-start.1
  2.3 1.1 %collective-permute-done.other_grad_ref = bf16[32,4096]{1,0:T(8,128)(2,1)S(1)} collective-permute-done((bf16[32,4096]{1,0:T(8,128)(2,1)}, bf16[32,4096]{1,0:T(8,128)(2,1)S(1)}, u32[]{:S(2)}, u32[]{:S(2)}) %collective-permute-start) | collective-permute-done | bytes 262176 | tf_op jit(solution)/shard_map/ppermute | solution.py:42
  3.3 2.9 %collective-permute-start.2 = (f32[16,128]{1,0:T(8,128)S(1)}, f32[16,128]{1,0:T(8,128)S(1)}, u32[]{:S(2)}, u32[]{:S(2)}) collective-permute-start(f32[16,128]{1,0:T(8,128)S(1)} %shard_map.85.refs_0_), channel_id=1, source_target_pairs={{0,16},{1,25},{2,18},{3,27},{4,20},{5,29},{6,22},{7,31},{8,24},{9,... | collective-permute-start | bytes 24584 | tf_op jit(solution)/shard_map/ppermute | solution.py:331
  6.3 1.5 %collective-permute-start.1 = (f32[16,128]{1,0:T(8,128)S(1)}, f32[16,128]{1,0:T(8,128)S(1)}, u32[]{:S(2)}, u32[]{:S(2)}) collective-permute-start(f32[16,128]{1,0:T(8,128)S(1)} %shard_map.85.refs_0_), channel_id=1, source_target_pairs={{0,8},{8,0},{16,24},{24,16},{1,9},{9,1},{17,25},{25,17},{2,10},{10... | collective-permute-start | bytes 24584 | tf_op jit(solution)/shard_map/ppermute | solution.py:42
  7.8 0.1 collective-permute-done.2.refs_2_
  7.9 0.2 collective-permute-start.3
  8.1 0.0 collective-permute-done.4.other_error_ref
  8.1 0.0 copy-done.2
  8.1 0.0 copy-done.3
  8.1 0.0 copy-done.1
  8.1 0.0 copy-start.5
  8.1 0.3 %shard_map.86 = (f32[32,4096]{1,0:T(8,128)S(1)}, f32[16,4096]{1,0:T(8,128)S(1)}, f32[16,4096]{1,0:T(8,128)S(1)}, f32[16,4096]{1,0:T(8,128)S(1)}, f32[16,4096]{1,0:T(8,128)S(1)}) custom-call(f32[32,4096]{1,0:T(8,128)S(1)} %bitcast.13, f32[32,4096]{1,0:T(8,128)S(1)} %bitcast.15, f32[32,4096]{1,0:T(8,128)S(1)} %collective-permute-done.4.other_error_ref, ...), custom_call_target="tpu_custom_call" | custom-call | flops 524288 | bytes 3670016 | tf_op jit(solution)/shard_map/pallas_call | solution.py:129
  8.5 1.4 %collective-permute-done.1.refs_1_ = f32[16,128]{1,0:T(8,128)S(1)} collective-permute-done((f32[16,128]{1,0:T(8,128)S(1)}, f32[16,128]{1,0:T(8,128)S(1)}, u32[]{:S(2)}, u32[]{:S(2)}) %collective-permute-start.1) | collective-permute-done | bytes 8224 | tf_op jit(solution)/shard_map/ppermute | solution.py:42
  9.9 0.0 collective-permute-done.3.refs_3_
  9.9 0.0 copy-done.5
  9.9 0.4 %shard_map.87 = (bf16[8,4096]{1,0:T(8,128)(2,1)S(1)}, bf16[8,4096]{1,0:T(8,128)(2,1)S(1)}, f32[8,128]{1,0:T(8,128)S(1)}) custom-call(f32[16,128]{1,0:T(8,128)S(1)} %shard_map.85.refs_0_, f32[16,128]{1,0:T(8,128)S(1)} %collective-permute-done.1.refs_1_, f32[16,128]{1,0:T(8,128)S(1)} %collective-permute-done.2.refs_2_, ...), custom_call_target="tpu_custom_call" | custom-call | flops 2621440 | bytes 1282048 | tf_op jit(solution)/shard_map/pallas_call | solution.py:129
  10.3 0.0 copy-start.4
  10.3 2.7 %collective-permute-start.7 = (bf16[8,4096]{1,0:T(8,128)(2,1)S(1)}, bf16[8,4096]{1,0:T(8,128)(2,1)S(1)}, u32[]{:S(2)}, u32[]{:S(2)}) collective-permute-start(bf16[8,4096]{1,0:T(8,128)(2,1)S(1)} %get-tuple-element.24.own_ref), channel_id=1, source_target_pairs={{0,4},{1,5},{2,6},{3,7},{4,0},{5,1},{6,2},{7,3},{8,12},{9,13},{10,... | collective-permute-start | bytes 196616 | tf_op jit(solution)/shard_map/ppermute | solution.py:42
  13.0 1.3 %collective-permute-start.6 = (bf16[8,4096]{1,0:T(8,128)(2,1)S(1)}, bf16[8,4096]{1,0:T(8,128)(2,1)S(1)}, u32[]{:S(2)}, u32[]{:S(2)}) collective-permute-start(bf16[8,4096]{1,0:T(8,128)(2,1)S(1)} %get-tuple-element.25), channel_id=1, source_target_pairs={{0,6},{1,7},{2,4},{3,5},{4,2},{5,3},{6,0},{7,1},{8,14},{9,15},{10,... | collective-permute-start | bytes 196616 | tf_op jit(solution)/shard_map/ppermute | solution.py:42
  14.3 0.2 collective-permute-start.5
  14.6 3.3 %collective-permute-done.7.across_ref = bf16[8,4096]{1,0:T(8,128)(2,1)S(1)} collective-permute-done((bf16[8,4096]{1,0:T(8,128)(2,1)S(1)}, bf16[8,4096]{1,0:T(8,128)(2,1)S(1)}, u32[]{:S(2)}, u32[]{:S(2)}) %collective-permute-start.7) | collective-permute-done | bytes 65568 | tf_op jit(solution)/shard_map/ppermute | solution.py:42
  17.9 1.3 %collective-permute-done.6.far_ref = bf16[8,4096]{1,0:T(8,128)(2,1)S(1)} collective-permute-done((bf16[8,4096]{1,0:T(8,128)(2,1)S(1)}, bf16[8,4096]{1,0:T(8,128)(2,1)S(1)}, u32[]{:S(2)}, u32[]{:S(2)}) %collective-permute-start.6) | collective-permute-done | bytes 65568 | tf_op jit(solution)/shard_map/ppermute | solution.py:42
  19.2 0.2 collective-permute-done.5.near_ref
  19.4 0.2 shard_map.88
  19.6 0.1 collective-permute-start.10
  19.6 1.0 %collective-permute-start.9 = (bf16[8,4096]{1,0:T(8,128)(2,1)S(1)}, bf16[8,4096]{1,0:T(8,128)(2,1)S(1)}, u32[]{:S(2)}, u32[]{:S(2)}) collective-permute-start(bf16[8,4096]{1,0:T(8,128)(2,1)S(1)} %get-tuple-element.26.mine_ref), channel_id=1, source_target_pairs={{0,3},{1,2},{2,1},{3,0},{4,7},{5,6},{6,5},{7,4},{8,11},{9,10},{10,... | collective-permute-start | bytes 196616 | tf_op jit(solution)/shard_map/ppermute | solution.py:367
  20.6 1.1 %collective-permute-start.8 = (bf16[8,4096]{1,0:T(8,128)(2,1)S(1)}, bf16[8,4096]{1,0:T(8,128)(2,1)S(1)}, u32[]{:S(2)}, u32[]{:S(2)}) collective-permute-start(bf16[8,4096]{1,0:T(8,128)(2,1)S(1)} %get-tuple-element.26.mine_ref), channel_id=1, source_target_pairs={{0,2},{1,3},{2,0},{3,1},{4,6},{5,7},{6,4},{7,5},{8,10},{9,11},{10,... | collective-permute-start | bytes 196616 | tf_op jit(solution)/shard_map/ppermute | solution.py:42
  21.8 0.0 copy-done.4
  21.8 1.0 %shard_map.89 = (f32[32,4096]{1,0:T(8,128)}, f32[32,4096]{1,0:T(8,128)S(1)}) custom-call(f32[8,128]{1,0:T(8,128)S(1)} %get-tuple-element.27.gain_ref, bf16[32,4096]{1,0:T(8,128)(2,1)S(1)} %bitcast.12, f32[32,4096]{1,0:T(8,128)S(1)} %get-tuple-element.28.base_ref, bf16[32,4096]{1,0:T(8,128)(2,1)S(1)} %bitcast.16), custom_call_target="tpu_custom_call" | custom-call | flops 2621440 | bytes 2101248 | tf_op jit(solution)/shard_map/pallas_call | solution.py:129
  22.8 0.8 %shard_map.92 = f32[4,4096]{1,0:T(4,128)} custom-call(f32[8,4096]{1,0:T(8,128)S(1)} %get-tuple-element.35.sum_ref), custom_call_target="tpu_custom_call" | custom-call | flops 655360 | bytes 196608 | tf_op jit(solution)/shard_map/pallas_call | solution.py:129
  23.6 0.0 collective-permute-done.10.other_ref
  23.6 0.8 %shard_map.90 = (f32[32,4096]{1,0:T(8,128)}, bf16[32,4096]{1,0:T(8,128)(2,1)}) custom-call(bf16[8,4096]{1,0:T(8,128)(2,1)S(1)} %get-tuple-element.26.mine_ref, bf16[8,4096]{1,0:T(8,128)(2,1)S(1)} %collective-permute-done.10.other_ref, f32[32,4096]{1,0:T(8,128)S(1)} %get-tuple-element.29.inverse_ref), custom_call_target="tpu_custom_call" | custom-call | flops 262144 | bytes 1441792 | tf_op jit(solution)/shard_map/pallas_call | solution.py:129
  24.4 0.0 collective-permute-done.9.other_ref
  24.4 1.1 %collective-permute-done.8.mine_ref = bf16[8,4096]{1,0:T(8,128)(2,1)S(1)} collective-permute-done((bf16[8,4096]{1,0:T(8,128)(2,1)S(1)}, bf16[8,4096]{1,0:T(8,128)(2,1)S(1)}, u32[]{:S(2)}, u32[]{:S(2)}) %collective-permute-start.8) | collective-permute-done | bytes 65568 | tf_op jit(solution)/shard_map/ppermute | solution.py:42
  25.5 0.8 %shard_map.91 = (f32[32,4096]{1,0:T(8,128)}, bf16[32,4096]{1,0:T(8,128)(2,1)}) custom-call(bf16[8,4096]{1,0:T(8,128)(2,1)S(1)} %collective-permute-done.8.mine_ref, bf16[8,4096]{1,0:T(8,128)(2,1)S(1)} %collective-permute-done.9.other_ref, f32[32,4096]{1,0:T(8,128)S(1)} %get-tuple-element.29.inverse_ref, ...), custom_call_target="tpu_custom_call", output_to_operand_aliasing={{0}: (3, {}), {1}: (4, {})} | custom-call | flops 262144 | bytes 2228224 | tf_op jit(solution)/shard_map/pallas_call | solution.py:129
  (2 shorter events, 0.0 us)
Async XLA Ops:
  0.6 7.5 %collective-permute-start.4 = (f32[32,4096]{1,0:T(8,128)}, f32[32,4096]{1,0:T(8,128)S(1)}, u32[]{:S(2)}, u32[]{:S(2)}) collective-permute-start(f32[32,4096]{1,0:T(8,128)} %bitcast.14), channel_id=1, source_target_pairs={{0,1},{1,0},{2,3},{3,2},{4,5},{5,4},{6,7},{7,6},{8,9},{9,8},{10,11... | collective-permute-start | bytes 1572872 | tf_op jit(solution)/shard_map/ppermute | solution.py:42
  1.2 2.1 %collective-permute-start = (bf16[32,4096]{1,0:T(8,128)(2,1)}, bf16[32,4096]{1,0:T(8,128)(2,1)S(1)}, u32[]{:S(2)}, u32[]{:S(2)}) collective-permute-start(bf16[32,4096]{1,0:T(8,128)(2,1)} %bitcast.9), channel_id=1, source_target_pairs={{0,1},{1,0},{2,3},{3,2},{4,5},{5,4},{6,7},{7,6},{8,9},{9,8},{10,11... | collective-permute-start | bytes 786440 | tf_op jit(solution)/shard_map/ppermute | solution.py:42
  1.3 0.9 %copy-start = (bf16[1,1,32,4096]{3,2,1,0:T(8,128)(2,1)S(1)}, bf16[1,1,32,4096]{3,2,1,0:T(8,128)(2,1)}, u32[]{:S(2)}) copy-start(bf16[1,1,32,4096]{3,2,1,0:T(8,128)(2,1)} %param.5) | copy-start | bytes 786436
  2.2 5.9 %copy-start.2 = (f32[1,32,4096]{2,1,0:T(8,128)S(1)}, f32[1,32,4096]{2,1,0:T(8,128)}, u32[]{:S(2)}) copy-start(f32[1,32,4096]{2,1,0:T(8,128)} %param.6) | copy-start | bytes 1572868
  2.2 5.9 %copy-start.3 = (f32[1,1,32,4096]{3,2,1,0:T(8,128)S(1)}, f32[1,1,32,4096]{3,2,1,0:T(8,128)}, u32[]{:S(2)}) copy-start(f32[1,1,32,4096]{3,2,1,0:T(8,128)} %param.8) | copy-start | bytes 1572868
  2.2 5.9 %copy-start.1 = (bf16[1,1,32,4096]{3,2,1,0:T(8,128)(2,1)S(1)}, bf16[1,1,32,4096]{3,2,1,0:T(8,128)(2,1)}, u32[]{:S(2)}) copy-start(bf16[1,1,32,4096]{3,2,1,0:T(8,128)(2,1)} %param.5) | copy-start | bytes 786436
  3.3 4.6 %collective-permute-start.2 = (f32[16,128]{1,0:T(8,128)S(1)}, f32[16,128]{1,0:T(8,128)S(1)}, u32[]{:S(2)}, u32[]{:S(2)}) collective-permute-start(f32[16,128]{1,0:T(8,128)S(1)} %shard_map.85.refs_0_), channel_id=1, source_target_pairs={{0,16},{1,25},{2,18},{3,27},{4,20},{5,29},{6,22},{7,31},{8,24},{9,... | collective-permute-start | bytes 24584 | tf_op jit(solution)/shard_map/ppermute | solution.py:331
  6.3 3.7 %collective-permute-start.1 = (f32[16,128]{1,0:T(8,128)S(1)}, f32[16,128]{1,0:T(8,128)S(1)}, u32[]{:S(2)}, u32[]{:S(2)}) collective-permute-start(f32[16,128]{1,0:T(8,128)S(1)} %shard_map.85.refs_0_), channel_id=1, source_target_pairs={{0,8},{8,0},{16,24},{24,16},{1,9},{9,1},{17,25},{25,17},{2,10},{10... | collective-permute-start | bytes 24584 | tf_op jit(solution)/shard_map/ppermute | solution.py:42
  7.9 2.0 %collective-permute-start.3 = (f32[16,128]{1,0:T(8,128)S(1)}, f32[16,128]{1,0:T(8,128)S(1)}, u32[]{:S(2)}, u32[]{:S(2)}) collective-permute-start(f32[16,128]{1,0:T(8,128)S(1)} %collective-permute-done.2.refs_2_), channel_id=1, source_target_pairs={{0,1},{1,0},{2,3},{3,2},{4,5},{5,4},{6,7},{7,6},{8,9},{9,8},{10,11... | collective-permute-start | bytes 24584 | tf_op jit(solution)/shard_map/ppermute | solution.py:42
  8.1 1.8 %copy-start.5 = (f32[1,4,4096]{2,1,0:T(4,128)S(1)}, f32[1,4,4096]{2,1,0:T(4,128)}, u32[]{:S(2)}) copy-start(f32[1,4,4096]{2,1,0:T(4,128)} %param.9) | copy-start | bytes 196612
  10.3 11.4 %copy-start.4 = (bf16[1,32,4096]{2,1,0:T(8,128)(2,1)S(1)}, bf16[1,32,4096]{2,1,0:T(8,128)(2,1)}, u32[]{:S(2)}) copy-start(bf16[1,32,4096]{2,1,0:T(8,128)(2,1)} %param.7) | copy-start | bytes 786436
  10.3 7.5 %collective-permute-start.7 = (bf16[8,4096]{1,0:T(8,128)(2,1)S(1)}, bf16[8,4096]{1,0:T(8,128)(2,1)S(1)}, u32[]{:S(2)}, u32[]{:S(2)}) collective-permute-start(bf16[8,4096]{1,0:T(8,128)(2,1)S(1)} %get-tuple-element.24.own_ref), channel_id=1, source_target_pairs={{0,4},{1,5},{2,6},{3,7},{4,0},{5,1},{6,2},{7,3},{8,12},{9,13},{10,... | collective-permute-start | bytes 196616 | tf_op jit(solution)/shard_map/ppermute | solution.py:42
  13.0 6.2 %collective-permute-start.6 = (bf16[8,4096]{1,0:T(8,128)(2,1)S(1)}, bf16[8,4096]{1,0:T(8,128)(2,1)S(1)}, u32[]{:S(2)}, u32[]{:S(2)}) collective-permute-start(bf16[8,4096]{1,0:T(8,128)(2,1)S(1)} %get-tuple-element.25), channel_id=1, source_target_pairs={{0,6},{1,7},{2,4},{3,5},{4,2},{5,3},{6,0},{7,1},{8,14},{9,15},{10,... | collective-permute-start | bytes 196616 | tf_op jit(solution)/shard_map/ppermute | solution.py:42
  14.3 5.0 %collective-permute-start.5 = (bf16[8,4096]{1,0:T(8,128)(2,1)S(1)}, bf16[8,4096]{1,0:T(8,128)(2,1)S(1)}, u32[]{:S(2)}, u32[]{:S(2)}) collective-permute-start(bf16[8,4096]{1,0:T(8,128)(2,1)S(1)} %get-tuple-element.25), channel_id=1, source_target_pairs={{0,2},{1,3},{2,0},{3,1},{4,6},{5,7},{6,4},{7,5},{8,10},{9,11},{10,... | collective-permute-start | bytes 196616 | tf_op jit(solution)/shard_map/ppermute | solution.py:42
  19.6 4.0 %collective-permute-start.10 = (bf16[8,4096]{1,0:T(8,128)(2,1)S(1)}, bf16[8,4096]{1,0:T(8,128)(2,1)S(1)}, u32[]{:S(2)}, u32[]{:S(2)}) collective-permute-start(bf16[8,4096]{1,0:T(8,128)(2,1)S(1)} %get-tuple-element.26.mine_ref), channel_id=1, source_target_pairs={{0,1},{1,0},{2,3},{3,2},{4,5},{5,4},{6,7},{7,6},{8,9},{9,8},{10,11... | collective-permute-start | bytes 196616 | tf_op jit(solution)/shard_map/ppermute | solution.py:42
  19.6 4.8 %collective-permute-start.9 = (bf16[8,4096]{1,0:T(8,128)(2,1)S(1)}, bf16[8,4096]{1,0:T(8,128)(2,1)S(1)}, u32[]{:S(2)}, u32[]{:S(2)}) collective-permute-start(bf16[8,4096]{1,0:T(8,128)(2,1)S(1)} %get-tuple-element.26.mine_ref), channel_id=1, source_target_pairs={{0,3},{1,2},{2,1},{3,0},{4,7},{5,6},{6,5},{7,4},{8,11},{9,10},{10,... | collective-permute-start | bytes 196616 | tf_op jit(solution)/shard_map/ppermute | solution.py:367
  20.6 4.9 %collective-permute-start.8 = (bf16[8,4096]{1,0:T(8,128)(2,1)S(1)}, bf16[8,4096]{1,0:T(8,128)(2,1)S(1)}, u32[]{:S(2)}, u32[]{:S(2)}) collective-permute-start(bf16[8,4096]{1,0:T(8,128)(2,1)S(1)} %get-tuple-element.26.mine_ref), channel_id=1, source_target_pairs={{0,2},{1,3},{2,0},{3,1},{4,6},{5,7},{6,4},{7,5},{8,10},{9,11},{10,... | collective-permute-start | bytes 196616 | tf_op jit(solution)/shard_map/ppermute | solution.py:42
